TPU v7x, 128 devices: a whole 4x4x4 slice. The times are simulated.
128 devices in a mesh: corpus: 16 (over z, y), fsdp: 2 (over core), tensor: 4 (over x).
Axes of the slice: x: 4, y: 4, z: 4, core: 2. Of those that a mesh axis runs over, the one named last changes fastest.
Arguments:
- queries_in: bfloat16 [4096, 4096], P(('corpus', 'fsdp')), may hold values from -6 to 6
- head_weight: bfloat16 [4096, 4096], P('fsdp', 'tensor'), may hold values from -0.09375 to 0.09375
- passages: bfloat16 [16384, 4096], P('corpus', 'tensor'), may hold values from -0.15625 to 0.15625
- teacher: float32 [4096, 4, 32], P(('corpus', 'fsdp')), may hold values from -250 to 400
- cand_block: int32 [4096, 4], P(('corpus', 'fsdp')), may hold values from 0 to 127, all different within a row; in each aligned block of 128 rows (0 to 127, 128 to 255, ...) at most 6 rows name the same one
- cand_offset: int32 [4096, 4, 32], P(('corpus', 'fsdp')), may hold values from 0 to 127, as said below
- block_slot: int32 [128], replicated, may hold values from 0 to 127, each once
Outputs:
- kl_loss: float32 [4096], P(('corpus', 'fsdp'))
- head_grad: float32 [4096, 4096], P('fsdp', 'tensor')
Inputs may be any that keep to these rules, and one draw needn't show every extreme that they name: `cand_block`: in the rows of one device no block id appears more than 6 times, and some block id appears exactly 6 times there; the 4 ids of one query differ. `cand_offset`: the 32 offsets of one query in one block differ. `block_slot`: each storage position is taken by exactly one block.
All inputs are finite; a program needn't handle non-finite values.
Results may differ from a plain program's by a relative error of at most 0.012.
The roundings to bfloat16 on the way count: a program that leaves them out, or rounds other values in their place, can miss the bound.
Values may be sent and summed in bfloat16 or wider, within the bound.
A program may use at most 128 MiB of HBM per device.

v0:
```python
import jax
import jax.numpy as jnp
from jax import lax
from jax.sharding import PartitionSpec as P

ROWS = 128
MOSTB = 6
SWAP = [(0, 1), (1, 0)]


def on_device(queries_in, head_weight, passages, teacher, cand_block, cand_offset, block_slot):
    query_rows, width = queries_in.shape
    half = width // 2
    cols = head_weight.shape[1]
    per_query = cand_block.shape[1]
    offset_count = cand_offset.shape[2]
    total_blocks = block_slot.shape[0]
    n_corpus = lax.axis_size("corpus")
    blocks_here = passages.shape[0] // ROWS
    slot_total = total_blocks * MOSTB
    slots_each = blocks_here * MOSTB
    picks = query_rows * per_query
    first = lax.axis_index("fsdp") == 0
    low, high = (queries_in[:, :half], queries_in[:, half:])
    mine = jnp.where(first, low, high)
    other = jnp.where(first, high, low)
    theirs = lax.ppermute(other, "fsdp", SWAP)
    part_theirs = jnp.dot(theirs, head_weight, preferred_element_type=jnp.float32)
    back = lax.ppermute(part_theirs, "fsdp", SWAP)
    part_mine = jnp.dot(mine, head_weight, preferred_element_type=jnp.float32)
    query = (part_mine + back).astype(jnp.bfloat16)
    all_mine = lax.all_gather(mine, "corpus", axis=0, tiled=True)
    all_theirs = lax.all_gather(theirs, "corpus", axis=0, tiled=True)
    block_ids = lax.broadcasted_iota(jnp.int32, (1, total_blocks), 1)
    named = (cand_block.reshape(-1, 1) == block_ids).astype(jnp.int32)
    slot_of = jnp.sum(named * block_slot.reshape(1, -1), axis=1)
    hits = slot_of[:, None] == block_ids
    before = (
        lax.broadcasted_iota(jnp.int32, (picks, picks), 1)
        < lax.broadcasted_iota(jnp.int32, (picks, picks), 0)
    ).astype(jnp.bfloat16)
    earlier = jnp.dot(before, hits.astype(jnp.bfloat16), preferred_element_type=jnp.float32)
    slot_rank = jnp.sum(jnp.where(hits, earlier, 0.0), axis=1).astype(jnp.int32)
    position = slot_of * MOSTB + slot_rank
    slot_ids = lax.broadcasted_iota(jnp.int32, (slot_total, 1), 0)
    place = (slot_ids == position.reshape(1, -1)).astype(jnp.bfloat16)
    by_query = position.reshape(query_rows, per_query)
    owner = slot_ids == by_query[:, 0].reshape(1, -1)
    for g in range(1, per_query):
        owner = owner | (slot_ids == by_query[:, g].reshape(1, -1))
    owner = owner.astype(jnp.bfloat16)
    slot_block = slot_ids % slots_each // MOSTB
    send_queries = jnp.dot(owner, query, preferred_element_type=jnp.float32).astype(jnp.bfloat16)
    got_queries = lax.all_to_all(
        send_queries.reshape(n_corpus, slots_each, cols), "corpus", 0, 0, tiled=True
    ).reshape(slot_total, cols)
    wide = lax.dot_general(
        got_queries, passages, (((1,), (1,)), ((), ())), preferred_element_type=jnp.float32
    )
    scores = wide[:, :ROWS]
    for j in range(1, blocks_here):
        scores = jnp.where(slot_block == j, wide[:, j * ROWS : (j + 1) * ROWS], scores)
    returned = lax.all_to_all(
        scores.reshape(n_corpus, slots_each, ROWS), "corpus", 0, 0, tiled=True
    ).reshape(slot_total, ROWS)
    picked = returned[position]
    offsets = cand_offset.reshape(picks, offset_count)
    row_ids = lax.broadcasted_iota(jnp.int32, (1, 1, ROWS), 2)
    chosen = offsets[:, :, None] == row_ids
    partial = jnp.sum(jnp.where(chosen, picked[:, None, :], 0.0), axis=2)
    total = partial.reshape(query_rows, per_query * offset_count)
    total = total + lax.ppermute(total, "tensor", [(0, 1), (1, 0), (2, 3), (3, 2)])
    total = total + lax.ppermute(total, "tensor", [(0, 2), (2, 0), (1, 3), (3, 1)])
    student = 50.0 * total
    cached = teacher.reshape(query_rows, per_query * offset_count)
    log_student = student - jax.nn.logsumexp(student, axis=1, keepdims=True)
    log_teacher = cached - jax.nn.logsumexp(cached, axis=1, keepdims=True)
    prob_teacher = jnp.exp(log_teacher)
    kl_loss = jnp.sum(prob_teacher * (log_teacher - log_student), axis=1)
    dscore = (50.0 * (jnp.exp(log_student) - prob_teacher)).astype(jnp.bfloat16)
    spread = jnp.sum(
        jnp.where(chosen, dscore.reshape(picks, offset_count, 1).astype(jnp.float32), 0.0), axis=1
    ).astype(jnp.bfloat16)
    dense = jnp.dot(place, spread, preferred_element_type=jnp.float32).astype(jnp.bfloat16)
    got_dense = lax.all_to_all(
        dense.reshape(n_corpus, slots_each, ROWS), "corpus", 0, 0, tiled=True
    ).reshape(slot_total, ROWS)
    expanded = jnp.concatenate(
        [jnp.where(slot_block == j, got_dense, jnp.bfloat16(0)) for j in range(blocks_here)], axis=1
    )
    block_part = jnp.dot(expanded, passages, preferred_element_type=jnp.float32).astype(
        jnp.bfloat16
    )
    arrived = lax.all_to_all(
        block_part.reshape(n_corpus, slots_each, cols), "corpus", 0, 0, tiled=True
    ).reshape(slot_total, cols)
    query_grad = lax.dot_general(
        owner, arrived, (((0,), (0,)), ((), ())), preferred_element_type=jnp.float32
    ).astype(jnp.bfloat16)
    grad_mine = lax.all_gather(query_grad, "corpus", axis=0, tiled=True)
    grad_theirs = lax.ppermute(grad_mine, "fsdp", SWAP)
    across = (((0,), (0,)), ((), ()))
    head_grad = lax.dot_general(
        all_mine, grad_mine, across, preferred_element_type=jnp.float32
    ) + lax.dot_general(all_theirs, grad_theirs, across, preferred_element_type=jnp.float32)
    return (kl_loss, head_grad)


def solution(mesh):
    placed = (
        P(("corpus", "fsdp"), None),
        P("fsdp", "tensor"),
        P("corpus", "tensor"),
        P(("corpus", "fsdp"), None, None),
        P(("corpus", "fsdp"), None),
        P(("corpus", "fsdp"), None, None),
        P(),
    )
    return jax.shard_map(
        on_device,
        mesh=mesh,
        in_specs=placed,
        out_specs=(P(("corpus", "fsdp")), P("fsdp", "tensor")),
        check_vma=False,
    )
```

profile of v0, /device:TPU:1, one launch (start us, length us, event | category | flops | bytes accessed | tf_op | source)
XLA Modules:
  0.0 353.7 jit_solution(15698942265412292982)
XLA Ops:
  7.2 2.2 broadcast_select_fusion
  9.4 1.4 collective-permute-start
  10.8 0.1 copy.18
  10.9 0.1 eq.213
  11.0 1.5 collective-permute-done
  12.5 3.9 %fusion.26 = f32[128,1024]{1,0:T(8,128)} fusion(bf16[128,2048]{1,0:T(8,128)(2,1)S(1)} %collective-permute-done, bf16[2048,1024]{1,0:T(8,128)(2,1)} %param.8), kind=kOutput, calls=%fused_computation.91 | convolution fusion | flops 536870912 | bytes 5242880 | tf_op jit(solution)/shard_map/dot_general | solution.py:28
  16.5 0.4 collective-permute-start.1
  16.8 0.2 select_reduce_fusion.2
  17.1 0.3 fusion.2
  17.4 0.1 add.152
  17.5 0.2 slice_reduce_fusion.3
  17.8 1.0 collective-permute-done.1
  18.7 4.6 %convolution_convert_fusion = bf16[768,1024]{1,0:T(8,128)(2,1)} fusion(f32[128,1024]{1,0:T(8,128)} %collective-permute-done.1, s32[128]{0:T(128)S(1)} %get-tuple-element.3, s32[128]{0:T(128)S(1)} %get-tuple-element.4, s32[128]{0:T(128)S(1)} %get-tuple-element.5, s32[128]{0:T(128)S(1)} %get-tuple-element.2, bf16[128,2048]{1,0:T(8,128)(2,1)S(1)} %get-tuple-element.9, ...), kind=kOutput, calls=%fused_computation.5 | convolution fusion | flops 739934208 | bytes 6817792 | tf_op jit(solution)/shard_map/dot_general | solution.py:53
  23.3 7.9 %all-to-all-start = ((bf16[16,48,1024]{2,1,0:T(8,128)(2,1)}), bf16[16,48,1024]{2,1,0:T(8,128)(2,1)}, u32[]{:S(2)}, u32[]{:S(2)}) async-start(bf16[16,48,1024]{2,1,0:T(8,128)(2,1)} %bitcast.46), calls=%async_computation | async-start | bytes 3145728 | tf_op jit(solution)/shard_map/all_to_all | solution.py:54
  31.4 23.9 %all-to-all-done = bf16[16,48,1024]{2,1,0:T(8,128)(2,1)} async-done(((bf16[16,48,1024]{2,1,0:T(8,128)(2,1)}), bf16[16,48,1024]{2,1,0:T(8,128)(2,1)}, u32[]{:S(2)}, u32[]{:S(2)}) %all-to-all-start) | async-done | bytes 1572896 | tf_op jit(solution)/shard_map/all_to_all | solution.py:54
  55.3 3.2 fusion.27
  58.6 2.1 fusion.9
  60.7 4.1 %all-to-all-start.1 = ((f32[16,48,128]{2,1,0:T(8,128)}), f32[16,48,128]{2,1,0:T(8,128)S(1)}, u32[]{:S(2)}, u32[]{:S(2)}) async-start(f32[16,48,128]{2,1,0:T(8,128)} %bitcast.4), calls=%async_computation.1 | async-start | bytes 786432 | tf_op jit(solution)/shard_map/all_to_all | solution.py:63
  64.8 0.1 copy.17
  65.0 8.7 %all-to-all-done.1 = f32[16,48,128]{2,1,0:T(8,128)S(1)} async-done(((f32[16,48,128]{2,1,0:T(8,128)}), f32[16,48,128]{2,1,0:T(8,128)S(1)}, u32[]{:S(2)}, u32[]{:S(2)}) %all-to-all-start.1) | async-done | bytes 393248 | tf_op jit(solution)/shard_map/all_to_all | solution.py:63
  73.8 1.0 gather_fusion
  74.8 5.1 %select_reduce_fusion.1 = f32[512,32]{1,0:T(8,128)S(1)} fusion(f32[512,128]{1,0:T(8,128)S(1)} %gather_fusion, s32[512,32]{1,0:T(8,128)S(1)} %bitcast.47), kind=kLoop, calls=%fused_computation.2 | loop fusion | flops 6275072 | bytes 393216 | tf_op jit(solution)/shard_map/reduce_sum | solution.py:70
  79.9 0.1 reshape.196
  80.0 0.1 copy.20
  80.1 1.3 collective-permute-start.2
  81.5 1.9 collective-permute-done.2
  83.3 2.8 collective-permute-start.3
  86.2 2.6 collective-permute-done.3
  88.8 0.6 fusion.18
  89.4 0.1 copy.21
  89.5 0.1 reshape.201
  89.6 5.6 %select_reduce_fusion = bf16[512,128]{1,0:T(8,128)(2,1)S(1)} fusion(f32[512,32]{1,0:T(8,128)S(1)} %reshape.201, s32[512,32]{1,0:T(8,128)S(1)} %bitcast.48), kind=kLoop, calls=%fused_computation.1 | loop fusion | flops 6225920 | bytes 262144 | tf_op jit(solution)/shard_map/reduce_sum | solution.py:81
  95.2 1.1 fusion.1
  96.3 3.5 all-to-all-start.2
  99.9 7.1 %all-to-all-done.2 = bf16[16,48,128]{2,1,0:T(8,128)(2,1)S(1)} async-done(((bf16[16,48,128]{2,1,0:T(8,128)(2,1)}), bf16[16,48,128]{2,1,0:T(8,128)(2,1)S(1)}, u32[]{:S(2)}, u32[]{:S(2)}) %all-to-all-start.2) | async-done | bytes 196640 | tf_op jit(solution)/shard_map/all_to_all | solution.py:85
  107.0 1.2 bitcast_select_fusion
  108.4 0.1 constant_dynamic-update-slice_fusion.3
  108.7 1.8 convolution_convert_fusion.1
  110.5 21.1 %all_to_all.20 = bf16[16,48,1024]{2,1,0:T(8,128)(2,1)S(1)} all-to-all(bf16[16,48,1024]{2,1,0:T(8,128)(2,1)S(1)} %bitcast.50), channel_id=1, replica_groups=mesh['corpus'=16,'fsdp'=2,'tensor'=4] {'corpus'}, dimensions={0} | all-to-all | bytes 3145728 | tf_op jit(solution)/shard_map/all_to_all | solution.py:94
  131.6 1.2 convolution_convert_fusion.2
  132.9 0.7 all-gather.4.cloned.1.call-update
  133.6 0.7 all-gather.8.cloned.1.call-update
  134.3 51.5 %all-gather.6.cloned.1.call-done = bf16[2048,1024]{1,0:T(8,128)(2,1)} async-done(((bf16[128,1024]{1,0:T(8,128)(2,1)}), bf16[2048,1024]{1,0:T(8,128)(2,1)}) %all-gather.6.cloned.1.call-update) | async-done | bytes 4194320 | tf_op jit(solution)/shard_map/all_gather | solution.py:100
  185.8 0.8 collective-permute-start.4
  186.6 71.8 %all-gather.4.cloned.1.call-done = bf16[2048,2048]{1,0:T(8,128)(2,1)} async-done(((bf16[128,2048]{1,0:T(8,128)(2,1)}), bf16[2048,2048]{1,0:T(8,128)(2,1)}) %all-gather.4.cloned.1.call-update) | async-done | bytes 8388624 | tf_op jit(solution)/shard_map/all_gather | solution.py:32
  258.5 14.6 %fusion.28 = f32[2048,1024]{1,0:T(8,128)} fusion(bf16[2048,2048]{1,0:T(8,128)(2,1)} %all-gather.4.cloned.1.call-done, bf16[2048,1024]{1,0:T(8,128)(2,1)} %all-gather.6.cloned.1.call-done), kind=kOutput, calls=%fused_computation.93 | convolution fusion | flops 8589934592 | bytes 20971520 | tf_op jit(solution)/shard_map/dot_general | solution.py:103
  273.1 58.1 %all-gather.8.cloned.1.call-done = bf16[2048,2048]{1,0:T(8,128)(2,1)} async-done(((bf16[128,2048]{1,0:T(8,128)(2,1)}), bf16[2048,2048]{1,0:T(8,128)(2,1)}) %all-gather.8.cloned.1.call-update) | async-done | bytes 8388624 | tf_op jit(solution)/shard_map/all_gather | solution.py:33
  331.2 16.0 %convolution_add_fusion = f32[2048,1024]{1,0:T(8,128)} fusion(f32[2048,1024]{1,0:T(8,128)} %fusion.28, bf16[2048,2048]{1,0:T(8,128)(2,1)} %all-gather.8.cloned.1.call-done, bf16[2048,1024]{1,0:T(8,128)(2,1)} %collective-permute-done.4), kind=kOutput, calls=%fused_computation.4 | convolution fusion | flops 8592031744 | bytes 29360128 | tf_op jit(solution)/shard_map/dot_general | solution.py:105
  (45 shorter events, 0.9 us)
Async XLA Ops:
  7.2 48.1 %copy-start = (bf16[1024,1024]{1,0:T(8,128)(2,1)S(1)}, bf16[1024,1024]{1,0:T(8,128)(2,1)}, u32[]{:S(2)}) copy-start(bf16[1024,1024]{1,0:T(8,128)(2,1)} %param.9) | copy-start | bytes 6291460
  7.2 3.6 %copy-start.6 = (s32[128,4]{0,1:T(4,128)S(1)}, s32[128,4]{0,1:T(4,128)}, u32[]{:S(2)}) copy-start(s32[128,4]{0,1:T(4,128)} %param.11) | copy-start | bytes 6148
  9.4 9.3 %copy-start.2 = (bf16[128,2048]{1,0:T(8,128)(2,1)}, bf16[128,2048]{1,0:T(8,128)(2,1)S(1)}, u32[]{:S(2)}) copy-start(bf16[128,2048]{1,0:T(8,128)(2,1)S(1)} %get-tuple-element.9) | copy-start | bytes 1572868
  9.4 3.1 collective-permute-start
  12.5 3.9 %copy-start.3 = (bf16[128,2048]{1,0:T(8,128)(2,1)}, bf16[128,2048]{1,0:T(8,128)(2,1)S(1)}, u32[]{:S(2)}) copy-start(bf16[128,2048]{1,0:T(8,128)(2,1)S(1)} %collective-permute-done) | copy-start | bytes 1572868
  12.5 4.3 %copy-start.7 = (s32[128]{0:T(128)S(1)}, s32[128]{0:T(128)}, u32[]{:S(2)}) copy-start(s32[128]{0:T(128)} %param.13) | copy-start | bytes 1540
  16.5 2.3 collective-permute-start.1
  23.3 32.0 %all-to-all-start = ((bf16[16,48,1024]{2,1,0:T(8,128)(2,1)}), bf16[16,48,1024]{2,1,0:T(8,128)(2,1)}, u32[]{:S(2)}, u32[]{:S(2)}) async-start(bf16[16,48,1024]{2,1,0:T(8,128)(2,1)} %bitcast.46), calls=%async_computation | async-start | bytes 3145728 | tf_op jit(solution)/shard_map/all_to_all | solution.py:54
  58.5 6.2 %copy-start.5 = (s32[128,4,32]{0,2,1:T(8,128)S(1)}, s32[128,4,32]{0,2,1:T(8,128)}, u32[]{:S(2)}) copy-start(s32[128,4,32]{0,2,1:T(8,128)} %param.12) | copy-start | bytes 196612
  58.6 6.4 %copy-start.4 = (f32[128,4,32]{0,2,1:T(8,128)S(1)}, f32[128,4,32]{0,2,1:T(8,128)}, u32[]{:S(2)}) copy-start(f32[128,4,32]{0,2,1:T(8,128)} %param.10) | copy-start | bytes 196612
  60.7 13.1 %all-to-all-start.1 = ((f32[16,48,128]{2,1,0:T(8,128)}), f32[16,48,128]{2,1,0:T(8,128)S(1)}, u32[]{:S(2)}, u32[]{:S(2)}) async-start(f32[16,48,128]{2,1,0:T(8,128)} %bitcast.4), calls=%async_computation.1 | async-start | bytes 786432 | tf_op jit(solution)/shard_map/all_to_all | solution.py:63
  80.1 3.2 collective-permute-start.2
  83.3 5.4 %collective-permute-start.3 = (f32[128,128]{0,1:T(8,128)S(1)}, f32[128,128]{0,1:T(8,128)S(1)}, u32[]{:S(2)}, u32[]{:S(2)}) collective-permute-start(f32[128,128]{0,1:T(8,128)S(1)} %add.157), channel_id=1, source_target_pairs={{0,2},{2,0},{1,3},{3,1},{4,6},{6,4},{5,7},{7,5},{8,10},{10,8},{9,1... | collective-permute-start | bytes 196616 | tf_op jit(solution)/shard_map/ppermute | solution.py:73
  96.3 10.7 %all-to-all-start.2 = ((bf16[16,48,128]{2,1,0:T(8,128)(2,1)}), bf16[16,48,128]{2,1,0:T(8,128)(2,1)S(1)}, u32[]{:S(2)}, u32[]{:S(2)}) async-start(bf16[16,48,128]{2,1,0:T(8,128)(2,1)} %bitcast.8), calls=%async_computation.2 | async-start | bytes 393216 | tf_op jit(solution)/shard_map/all_to_all | solution.py:85
  99.8 85.9 %all-gather.6.cloned.1.call-start = ((), (), s32[]{:S(2)}) async-start(), calls=%async_computation.5 | async-start | bytes 4456448 | tf_op jit(solution)/shard_map/all_gather | solution.py:100
  132.8 125.6 %all-gather.4.cloned.1.call-start = ((), (), s32[]{:S(2)}) async-start(), calls=%async_computation.4 | async-start | bytes 8912896 | tf_op jit(solution)/shard_map/all_gather | solution.py:32
  133.6 197.6 %all-gather.8.cloned.1.call-start = ((), (), s32[]{:S(2)}) async-start(), calls=%async_computation.6 | async-start | bytes 8912896 | tf_op jit(solution)/shard_map/all_gather | solution.py:33
  185.8 145.4 %collective-permute-start.4 = (bf16[2048,1024]{1,0:T(8,128)(2,1)}, bf16[2048,1024]{1,0:T(8,128)(2,1)}, u32[]{:S(2)}, u32[]{:S(2)}) collective-permute-start(bf16[2048,1024]{1,0:T(8,128)(2,1)} %all-gather.6.cloned.1.call-done), channel_id=1, source_target_pairs={{0,4},{4,0},{1,5},{5,1},{2,6},{6,2},{3,7},{7,3},{8,12},{12,8},{9,1... | collective-permute-start | bytes 12582920 | tf_op jit(solution)/shard_map/ppermute | solution.py:101
  331.2 16.0 %copy-start.1 = (bf16[1024,1024]{1,0:T(8,128)(2,1)S(1)}, bf16[1024,1024]{1,0:T(8,128)(2,1)}, u32[]{:S(2)}) copy-start(bf16[1024,1024]{1,0:T(8,128)(2,1)} %param.9) | copy-start | bytes 6291460
Sparse Core Ops, SparseCore 0:
  132.9 52.7 all-gather.5
  187.9 70.5 all-gather.3
  260.6 70.5 all-gather.7
where the time goes:
time: 354 us
  waiting for transfers between devices  229 us (65%)
  matrix products  46.7 us (13%)
  starting transfers between devices  22.4 us (6%)
  blocking collectives  21.1 us (6%)
  other arithmetic  17.3 us (5%)
  between operations  14 us (4%)
    all_gather x1, waiting for transfers between devices, on_device(): all_mine = lax.all_gather(mine, 'corpus', axis=0, tiled=True)  71.8 us
    all_gather x1, waiting for transfers between devices, on_device(): all_theirs = lax.all_gather(theirs, 'corpus', axis=0, tiled=True)  58.1 us
    all_gather x1, waiting for transfers between devices, on_device(): grad_mine = lax.all_gather(query_grad, 'corpus', axis=0, tiled=True)  51.5 us
    all_to_all x1, waiting for transfers between devices, on_device(): lax.all_to_all(send_queries.reshape(n_corpus, slots_each, cols), 'corpus'...  23.9 us
    all_to_all x1, blocking collectives, on_device(): lax.all_to_all(block_part.reshape(n_corpus, slots_each, cols), 'corpus',...  21.1 us
    dot_general x1, matrix products, on_device(): lax.dot_general(all_theirs, grad_theirs, across, preferred_element_type=j...  16 us
    dot_general x1, matrix products, on_device(): lax.dot_general(all_mine, grad_mine, across, preferred_element_type=jnp.f...  14.6 us
    all_to_all x1, waiting for transfers between devices, on_device(): lax.all_to_all(scores.reshape(n_corpus, slots_each, ROWS), 'corpus', 0, 0...  8.74 us
  transfers between devices with their start and end apart: 11, of which 10 were waited for; matrix products, arithmetic and copies ran while one was open for 5% of the time, Pallas kernels for 0%

commit v1 on v0

--- a/solution.py
+++ b/solution.py
@@ -2,6 +2,7 @@
 import jax.numpy as jnp
 from jax import lax
 from jax.sharding import PartitionSpec as P
+from jax.lax import all_to_all, axis_size
 
 ROWS = 128
 MOSTB = 6
@@ -97,7 +98,12 @@
     query_grad = lax.dot_general(
         owner, arrived, (((0,), (0,)), ((), ())), preferred_element_type=jnp.float32
     ).astype(jnp.bfloat16)
-    grad_mine = lax.all_gather(query_grad, "corpus", axis=0, tiled=True)
+    grad_mine = jnp.concatenate(
+        all_to_all(
+            jnp.stack([query_grad for _ in range(axis_size("corpus"))], axis=0), "corpus", 0, 0
+        ),
+        0,
+    )
     grad_theirs = lax.ppermute(grad_mine, "fsdp", SWAP)
     across = (((0,), (0,)), ((), ()))
     head_grad = lax.dot_general(

time: 354 us -> 273 us (0.77)
  waiting for transfers between devices: 229 us -> 53.8 us
  blocking collectives: 21.1 us -> 110 us
  starting transfers between devices: 22.4 us -> 27.2 us
    all_to_all x0 -> x1, blocking collectives: none -> 86.8 us  [on_device(): all_to_all(jnp.stack([query_grad for _ in range(axis_size('corpus'))], ax...]
    all_gather x1, waiting for transfers between devices: 71.8 us -> 0.01 us  [on_device(): all_mine = lax.all_gather(mine, 'corpus', axis=0, tiled=True)]
    all_gather x1, waiting for transfers between devices: 58.1 us -> 0.01 us  [on_device(): all_theirs = lax.all_gather(theirs, 'corpus', axis=0, tiled=True)]
    all_gather x1 -> x0, waiting for transfers between devices: 51.5 us -> none  [on_device(): grad_mine = lax.all_gather(query_grad, 'corpus', axis=0, tiled=True)]
    all_to_all x1, waiting for transfers between devices: 8.74 us -> 13.9 us  [on_device(): lax.all_to_all(scores.reshape(n_corpus, slots_each, ROWS), 'corpus', 0, 0...]
  transfers between devices with their start and end apart: 11 -> 10, of which waited for: 10 -> 7; matrix products, arithmetic and copies ran while one was open for 5% -> 18% of each run, Pallas kernels for 0% -> 0%
where the time goes in v1:
time: 273 us; the launch traced here: 272 us
  blocking collectives  110 us (40%)
  waiting for transfers between devices  53.8 us (20%)
  matrix products  46 us (17%)
  starting transfers between devices  27.2 us (10%)
  other arithmetic  17.4 us (6%)
  between operations  14.3 us (5%)
  local copies, waits for them, and re-layouts  3.19 us (1%)
    all_to_all x1, blocking collectives, on_device(): all_to_all(jnp.stack([query_grad for _ in range(axis_size('corpus'))], ax...  86.8 us
    all_to_all x1, waiting for transfers between devices, on_device(): lax.all_to_all(send_queries.reshape(n_corpus, slots_each, cols), 'corpus'...  24.9 us
    all_to_all x1, blocking collectives, on_device(): lax.all_to_all(block_part.reshape(n_corpus, slots_each, cols), 'corpus',...  23.6 us
    dot_general x1, matrix products, on_device(): lax.dot_general(all_theirs, grad_theirs, across, preferred_element_type=j...  16 us
    dot_general x1, matrix products, on_device(): lax.dot_general(all_mine, grad_mine, across, preferred_element_type=jnp.f...  14.6 us
    all_to_all x1, waiting for transfers between devices, on_device(): lax.all_to_all(scores.reshape(n_corpus, slots_each, ROWS), 'corpus', 0, 0...  13.9 us
    all_to_all x1, starting transfers between devices, on_device(): lax.all_to_all(send_queries.reshape(n_corpus, slots_each, cols), 'corpus'...  7.92 us
    all_to_all x1, waiting for transfers between devices, on_device(): lax.all_to_all(dense.reshape(n_corpus, slots_each, ROWS), 'corpus', 0, 0,...  7.13 us
  transfers between devices with their start and end apart: 10, of which 7 were waited for; matrix products, arithmetic and copies ran while one was open for 18% of the time, Pallas kernels for 0%

profile of v1, /device:TPU:1, one launch (start us, length us, event | category | flops | bytes accessed | tf_op | source)
XLA Modules:
  0.0 272.2 jit_solution(5163541715565156069)
XLA Ops:
  7.2 2.3 broadcast_select_fusion
  9.5 1.5 collective-permute-start
  11.0 0.1 copy.18
  11.1 0.1 eq.213
  11.2 1.3 collective-permute-done
  12.5 3.9 %fusion.26 = f32[128,1024]{1,0:T(8,128)} fusion(bf16[128,2048]{1,0:T(8,128)(2,1)S(1)} %collective-permute-done, bf16[2048,1024]{1,0:T(8,128)(2,1)} %param.8), kind=kOutput, calls=%fused_computation.91 | convolution fusion | flops 536870912 | bytes 5242880 | tf_op jit(solution)/shard_map/dot_general | solution.py:29
  16.5 0.4 collective-permute-start.1
  16.9 0.2 select_reduce_fusion.2
  17.1 0.3 fusion.2
  17.4 0.1 add.152
  17.5 0.2 slice_reduce_fusion.3
  17.8 1.0 collective-permute-done.1
  18.7 4.6 %convolution_convert_fusion = bf16[768,1024]{1,0:T(8,128)(2,1)} fusion(f32[128,1024]{1,0:T(8,128)} %collective-permute-done.1, s32[128]{0:T(128)S(1)} %get-tuple-element.3, s32[128]{0:T(128)S(1)} %get-tuple-element.4, s32[128]{0:T(128)S(1)} %get-tuple-element.5, s32[128]{0:T(128)S(1)} %get-tuple-element.2, bf16[128,2048]{1,0:T(8,128)(2,1)S(1)} %copy-done.2, ...), kind=kOutput, calls=%fused_computation.5 | convolution fusion | flops 739934208 | bytes 6817792 | tf_op jit(solution)/shard_map/dot_general | solution.py:54
  23.3 7.9 %all-to-all-start = ((bf16[16,48,1024]{2,1,0:T(8,128)(2,1)}), bf16[16,48,1024]{2,1,0:T(8,128)(2,1)}, u32[]{:S(2)}, u32[]{:S(2)}) async-start(bf16[16,48,1024]{2,1,0:T(8,128)(2,1)} %bitcast.47), calls=%async_computation | async-start | bytes 3145728 | tf_op jit(solution)/shard_map/all_to_all | solution.py:55
  31.3 0.7 all-gather.5.cloned.1.call-update
  32.1 24.9 %all-to-all-done = bf16[16,48,1024]{2,1,0:T(8,128)(2,1)} async-done(((bf16[16,48,1024]{2,1,0:T(8,128)(2,1)}), bf16[16,48,1024]{2,1,0:T(8,128)(2,1)}, u32[]{:S(2)}, u32[]{:S(2)}) %all-to-all-start) | async-done | bytes 1572896 | tf_op jit(solution)/shard_map/all_to_all | solution.py:55
  57.0 3.2 %fusion.27 = f32[768,1024]{1,0:T(8,128)S(1)} fusion(bf16[768,1024]{1,0:T(8,128)(2,1)} %bitcast.3, bf16[1024,1024]{1,0:T(8,128)(2,1)S(1)} %copy-done), kind=kOutput, calls=%fused_computation.92 | convolution fusion | flops 1610612736 | bytes 6815744 | tf_op jit(solution)/shard_map/dot_general | solution.py:58
  60.3 2.1 fusion.9
  62.4 5.7 %all-to-all-start.1 = ((f32[16,48,128]{2,1,0:T(8,128)}), f32[16,48,128]{2,1,0:T(8,128)S(1)}, u32[]{:S(2)}, u32[]{:S(2)}) async-start(f32[16,48,128]{2,1,0:T(8,128)} %bitcast.4), calls=%async_computation.1 | async-start | bytes 786432 | tf_op jit(solution)/shard_map/all_to_all | solution.py:64
  68.1 0.1 copy.17
  68.3 13.9 %all-to-all-done.1 = f32[16,48,128]{2,1,0:T(8,128)S(1)} async-done(((f32[16,48,128]{2,1,0:T(8,128)}), f32[16,48,128]{2,1,0:T(8,128)S(1)}, u32[]{:S(2)}, u32[]{:S(2)}) %all-to-all-start.1) | async-done | bytes 393248 | tf_op jit(solution)/shard_map/all_to_all | solution.py:64
  82.2 1.0 gather_fusion
  83.2 5.1 %select_reduce_fusion.1 = f32[512,32]{1,0:T(8,128)S(1)} fusion(f32[512,128]{1,0:T(8,128)S(1)} %gather_fusion, s32[512,32]{1,0:T(8,128)S(1)} %bitcast.48), kind=kLoop, calls=%fused_computation.2 | loop fusion | flops 6275072 | bytes 393216 | tf_op jit(solution)/shard_map/reduce_sum | solution.py:71
  88.3 0.1 reshape.201
  88.4 0.1 copy.20
  88.5 1.2 collective-permute-start.2
  89.8 2.3 collective-permute-done.2
  92.2 2.6 collective-permute-start.3
  94.8 2.6 collective-permute-done.3
  97.5 0.6 fusion.18
  98.0 0.1 copy.21
  98.1 0.1 reshape.207
  98.3 5.6 %select_reduce_fusion = bf16[512,128]{1,0:T(8,128)(2,1)S(1)} fusion(f32[512,32]{1,0:T(8,128)S(1)} %reshape.207, s32[512,32]{1,0:T(8,128)S(1)} %bitcast.49), kind=kLoop, calls=%fused_computation.1 | loop fusion | flops 6225920 | bytes 262144 | tf_op jit(solution)/shard_map/reduce_sum | solution.py:82
  103.9 1.1 fusion.1
  105.0 3.5 %all-to-all-start.2 = ((bf16[16,48,128]{2,1,0:T(8,128)(2,1)}), bf16[16,48,128]{2,1,0:T(8,128)(2,1)S(1)}, u32[]{:S(2)}, u32[]{:S(2)}) async-start(bf16[16,48,128]{2,1,0:T(8,128)(2,1)} %bitcast.8), calls=%async_computation.2 | async-start | bytes 393216 | tf_op jit(solution)/shard_map/all_to_all | solution.py:86
  108.5 7.1 %all-to-all-done.2 = bf16[16,48,128]{2,1,0:T(8,128)(2,1)S(1)} async-done(((bf16[16,48,128]{2,1,0:T(8,128)(2,1)}), bf16[16,48,128]{2,1,0:T(8,128)(2,1)S(1)}, u32[]{:S(2)}, u32[]{:S(2)}) %all-to-all-start.2) | async-done | bytes 196640 | tf_op jit(solution)/shard_map/all_to_all | solution.py:86
  115.6 1.2 bitcast_select_fusion
  116.9 0.1 constant_dynamic-update-slice_fusion.6
  117.1 0.1 constant_dynamic-update-slice_fusion.3
  117.1 0.1 constant_dynamic-update-slice_fusion.2
  117.4 1.8 convolution_convert_fusion.1
  119.2 23.6 %all_to_all.25 = bf16[16,48,1024]{2,1,0:T(8,128)(2,1)S(1)} all-to-all(bf16[16,48,1024]{2,1,0:T(8,128)(2,1)S(1)} %bitcast.51), channel_id=1, replica_groups=mesh['corpus'=16,'fsdp'=2,'tensor'=4] {'corpus'}, dimensions={0} | all-to-all | bytes 3145728 | tf_op jit(solution)/shard_map/all_to_all | solution.py:95
  142.7 0.4 convolution_convert_fusion.2
  143.2 0.5 stack.2
  143.7 86.8 %all_to_all.26 = bf16[16,128,1024]{2,1,0:T(8,128)(2,1)} all-to-all(bf16[16,128,1024]{2,1,0:T(8,128)(2,1)S(1)} %stack.2), channel_id=1, replica_groups=mesh['corpus'=16,'fsdp'=2,'tensor'=4] {'corpus'}, dimensions={0} | all-to-all | bytes 8388608 | tf_op jit(solution)/shard_map/all_to_all | solution.py:102
  230.5 4.3 %collective-permute-start.4 = (bf16[2048,1024]{1,0:T(8,128)(2,1)}, bf16[2048,1024]{1,0:T(8,128)(2,1)}, u32[]{:S(2)}, u32[]{:S(2)}) collective-permute-start(bf16[2048,1024]{1,0:T(8,128)(2,1)} %bitcast.12), channel_id=1, source_target_pairs={{0,4},{4,0},{1,5},{5,1},{2,6},{6,2},{3,7},{7,3},{8,12},{12,8},{9,1... | collective-permute-start | bytes 12582920 | tf_op jit(solution)/shard_map/ppermute | solution.py:107
  234.8 14.6 %fusion.28 = f32[2048,1024]{1,0:T(8,128)} fusion(bf16[2048,2048]{1,0:T(8,128)(2,1)} %all-gather.3.cloned.1.call-done, bf16[2048,1024]{1,0:T(8,128)(2,1)} %bitcast.12), kind=kOutput, calls=%fused_computation.93 | convolution fusion | flops 8589934592 | bytes 20971520 | tf_op jit(solution)/shard_map/dot_general | solution.py:109
  249.4 16.0 %convolution_add_fusion = f32[2048,1024]{1,0:T(8,128)} fusion(f32[2048,1024]{1,0:T(8,128)} %fusion.28, bf16[2048,2048]{1,0:T(8,128)(2,1)} %all-gather.5.cloned.1.call-done, bf16[2048,1024]{1,0:T(8,128)(2,1)} %collective-permute-done.4), kind=kOutput, calls=%fused_computation.4 | convolution fusion | flops 8592031744 | bytes 29360128 | tf_op jit(solution)/shard_map/dot_general | solution.py:111
  (44 shorter events, 0.8 us)
Async XLA Ops:
  7.2 49.8 %copy-start = (bf16[1024,1024]{1,0:T(8,128)(2,1)S(1)}, bf16[1024,1024]{1,0:T(8,128)(2,1)}, u32[]{:S(2)}) copy-start(bf16[1024,1024]{1,0:T(8,128)(2,1)} %param.9) | copy-start | bytes 6291460
  7.2 3.8 %copy-start.6 = (s32[128,4]{0,1:T(4,128)S(1)}, s32[128,4]{0,1:T(4,128)}, u32[]{:S(2)}) copy-start(s32[128,4]{0,1:T(4,128)} %param.11) | copy-start | bytes 6148
  7.2 227.6 %all-gather.3.cloned.1.call-start = ((), (), s32[]{:S(2)}) async-start(), calls=%async_computation.5 | async-start | bytes 8912896 | tf_op jit(solution)/shard_map/all_gather | solution.py:33
  9.5 3.0 %collective-permute-start = (bf16[128,2048]{1,0:T(8,128)(2,1)S(1)}, bf16[128,2048]{1,0:T(8,128)(2,1)S(1)}, u32[]{:S(2)}, u32[]{:S(2)}) collective-permute-start(bf16[128,2048]{1,0:T(8,128)(2,1)S(1)} %get-tuple-element.8), channel_id=1, source_target_pairs={{0,4},{4,0},{1,5},{5,1},{2,6},{6,2},{3,7},{7,3},{8,12},{12,8},{9,1... | collective-permute-start | bytes 1572872 | tf_op jit(solution)/shard_map/ppermute | solution.py:28
  12.5 3.9 %copy-start.3 = (bf16[128,2048]{1,0:T(8,128)(2,1)}, bf16[128,2048]{1,0:T(8,128)(2,1)S(1)}, u32[]{:S(2)}) copy-start(bf16[128,2048]{1,0:T(8,128)(2,1)S(1)} %collective-permute-done) | copy-start | bytes 1572868
  12.5 4.3 %copy-start.7 = (s32[128]{0:T(128)S(1)}, s32[128]{0:T(128)}, u32[]{:S(2)}) copy-start(s32[128]{0:T(128)} %param.13) | copy-start | bytes 1540
  12.5 6.2 %copy-start.2 = (bf16[128,2048]{1,0:T(8,128)(2,1)S(1)}, bf16[128,2048]{1,0:T(8,128)(2,1)}, u32[]{:S(2)}) copy-start(bf16[128,2048]{1,0:T(8,128)(2,1)} %get-tuple-element.9) | copy-start | bytes 1572868
  16.5 2.3 collective-permute-start.1
  23.3 33.6 %all-to-all-start = ((bf16[16,48,1024]{2,1,0:T(8,128)(2,1)}), bf16[16,48,1024]{2,1,0:T(8,128)(2,1)}, u32[]{:S(2)}, u32[]{:S(2)}) async-start(bf16[16,48,1024]{2,1,0:T(8,128)(2,1)} %bitcast.47), calls=%async_computation | async-start | bytes 3145728 | tf_op jit(solution)/shard_map/all_to_all | solution.py:55
  31.3 218.1 %all-gather.5.cloned.1.call-start = ((), (), s32[]{:S(2)}) async-start(), calls=%async_computation.6 | async-start | bytes 8912896 | tf_op jit(solution)/shard_map/all_gather | solution.py:34
  60.2 7.8 %copy-start.5 = (s32[128,4,32]{0,2,1:T(8,128)S(1)}, s32[128,4,32]{0,2,1:T(8,128)}, u32[]{:S(2)}) copy-start(s32[128,4,32]{0,2,1:T(8,128)} %param.12) | copy-start | bytes 196612
  60.2 8.0 %copy-start.4 = (f32[128,4,32]{0,2,1:T(8,128)S(1)}, f32[128,4,32]{0,2,1:T(8,128)}, u32[]{:S(2)}) copy-start(f32[128,4,32]{0,2,1:T(8,128)} %param.10) | copy-start | bytes 196612
  62.4 19.8 %all-to-all-start.1 = ((f32[16,48,128]{2,1,0:T(8,128)}), f32[16,48,128]{2,1,0:T(8,128)S(1)}, u32[]{:S(2)}, u32[]{:S(2)}) async-start(f32[16,48,128]{2,1,0:T(8,128)} %bitcast.4), calls=%async_computation.1 | async-start | bytes 786432 | tf_op jit(solution)/shard_map/all_to_all | solution.py:64
  88.5 3.6 %collective-permute-start.2 = (f32[128,128]{0,1:T(8,128)S(1)}, f32[128,128]{0,1:T(8,128)S(1)}, u32[]{:S(2)}, u32[]{:S(2)}) collective-permute-start(f32[128,128]{0,1:T(8,128)S(1)} %copy.20), channel_id=1, source_target_pairs={{0,1},{1,0},{2,3},{3,2},{4,5},{5,4},{6,7},{7,6},{8,9},{9,8},{10,11... | collective-permute-start | bytes 196616 | tf_op jit(solution)/shard_map/ppermute | solution.py:73
  92.2 5.2 %collective-permute-start.3 = (f32[128,128]{0,1:T(8,128)S(1)}, f32[128,128]{0,1:T(8,128)S(1)}, u32[]{:S(2)}, u32[]{:S(2)}) collective-permute-start(f32[128,128]{0,1:T(8,128)S(1)} %add.157), channel_id=1, source_target_pairs={{0,2},{2,0},{1,3},{3,1},{4,6},{6,4},{5,7},{7,5},{8,10},{10,8},{9,1... | collective-permute-start | bytes 196616 | tf_op jit(solution)/shard_map/ppermute | solution.py:74
  105.0 10.7 %all-to-all-start.2 = ((bf16[16,48,128]{2,1,0:T(8,128)(2,1)}), bf16[16,48,128]{2,1,0:T(8,128)(2,1)S(1)}, u32[]{:S(2)}, u32[]{:S(2)}) async-start(bf16[16,48,128]{2,1,0:T(8,128)(2,1)} %bitcast.8), calls=%async_computation.2 | async-start | bytes 393216 | tf_op jit(solution)/shard_map/all_to_all | solution.py:86
  230.5 18.9 %collective-permute-start.4 = (bf16[2048,1024]{1,0:T(8,128)(2,1)}, bf16[2048,1024]{1,0:T(8,128)(2,1)}, u32[]{:S(2)}, u32[]{:S(2)}) collective-permute-start(bf16[2048,1024]{1,0:T(8,128)(2,1)} %bitcast.12), channel_id=1, source_target_pairs={{0,4},{4,0},{1,5},{5,1},{2,6},{6,2},{3,7},{7,3},{8,12},{12,8},{9,1... | collective-permute-start | bytes 12582920 | tf_op jit(solution)/shard_map/ppermute | solution.py:107
  249.4 16.0 %copy-start.1 = (bf16[1024,1024]{1,0:T(8,128)(2,1)S(1)}, bf16[1024,1024]{1,0:T(8,128)(2,1)}, u32[]{:S(2)}) copy-start(bf16[1024,1024]{1,0:T(8,128)(2,1)} %param.9) | copy-start | bytes 6291460
Sparse Core Ops, SparseCore 0:
  10.1 92.1 all-gather.2
  104.5 127.2 all-gather.4
